TPU v7x, 128 devices: a whole 4x4x4 slice. The times are simulated.
128 devices in a mesh: group: 8 (over y, core), local: 16 (over z, x).
Axes of the slice: x: 4, y: 4, z: 4, core: 2. Of those that a mesh axis runs over, the one named last changes fastest.
Arguments:
- lookup_grads: bfloat16 [1048576, 256], P(('group', 'local')), may hold values from -0.29882812 to 0.29882812
- slot_index: int32 [2, 1048576], P(None, ('group', 'local')), may hold values from 0 to 2047, as said below
- unique_rows: int32 [2, 16384], P(None, ('group', 'local')), may hold values from -1 to 131071, as said below
- tables: float32 [2, 131072, 256], P(None, ('group', 'local')), may hold values from -6 to 6
- accums: float32 [2, 131072], P(None, ('group', 'local')), may hold values from 0.01 to 1
Outputs:
- new_tables: float32 [2, 131072, 256], P(None, ('group', 'local'))
- new_accums: float32 [2, 131072], P(None, ('group', 'local'))
Inputs may be any that keep to these rules, and one draw needn't show every extreme that they name: slot_index[t, i] names a slot of lookup i's group list whose entry in unique_rows[t] is not -1. `unique_rows`: table row p is owned by device p // 1024, which is device (group p // 16384, local p // 1024 % 16). Group g's list is entries g * 2048 to (g + 1) * 2048 - 1; its block l of 128 entries consists of 8 buckets of 16 entries, bucket h holding only rows owned by device (group h, local l), the used entries first and -1 after them. Rows within a group's list are distinct. In every draw and table some device (group h, local l) gets a full bucket from every group.
All inputs are finite; a program needn't handle non-finite values.
Results may differ from a plain program's by a relative error of at most 0.0003.
Values sent between devices are 32-bit elements; how exact they have to be, the bound alone decides.
No kernel may reach another device: no remote copies, remote signals or barrier semaphores. Data moves between devices by JAX's collectives and lax.ppermute only.
A program may use at most 64 MiB of HBM per device.

v0:
```python
import jax
import jax.numpy as jnp
from jax import lax
from jax.sharding import PartitionSpec as P

learning_rate = 0.1
epsilon = 1e-08


def slot_sums(lookup_grads, slot_index, row_count):
    block_len = min(2048, lookup_grads.shape[0])
    block_count = lookup_grads.shape[0] // block_len
    width = lookup_grads.shape[1]
    grad_blocks = lookup_grads.reshape(block_count, block_len, width)
    index_blocks = jnp.transpose(slot_index.reshape(2, block_count, block_len), (1, 0, 2))
    targets = lax.iota(jnp.int32, row_count)

    def accumulate(running, inputs):
        gradients, indices = inputs
        pieces = []
        for table_index in range(2):
            onehot = (indices[table_index][:, None] == targets[None, :]).astype(jnp.bfloat16)
            pieces.append(
                lax.dot_general(
                    onehot, gradients, (((0,), (0,)), ((), ())), preferred_element_type=jnp.float32
                )
            )
        return (running + jnp.concatenate(pieces, axis=1), None)

    start_sums = jnp.zeros((row_count, 2 * width), jnp.float32)
    summed, _ = lax.scan(accumulate, start_sums, (grad_blocks, index_blocks))
    return summed


def apply_update(summed, row_pairs, tables, accums):
    rows_dev = tables.shape[1]
    width = tables.shape[2]
    new_tables = []
    new_accums = []
    for table_index in range(2):
        row_numbers = row_pairs[:, table_index]
        local_rows = jnp.where(row_numbers < 0, rows_dev, row_numbers % rows_dev)
        values = summed[:, table_index * width : (table_index + 1) * width]
        row_grads = (
            jnp.zeros((rows_dev, width), jnp.float32).at[local_rows].add(values, mode="drop")
        )
        accum_new = accums[table_index] + jnp.mean(row_grads * row_grads, axis=1)
        table_new = tables[table_index] - learning_rate * row_grads / (
            jnp.sqrt(accum_new)[:, None] + epsilon
        )
        new_tables.append(table_new)
        new_accums.append(accum_new)
    return (jnp.stack(new_tables), jnp.stack(new_accums))


def local(lookup_grads, slot_index, unique_rows, tables, accums):
    n_group = lax.axis_size("group")
    n_local = lax.axis_size("local")
    slots = unique_rows.shape[1]
    capacity = slots // n_group
    width = lookup_grads.shape[1]
    row_pairs = jnp.transpose(unique_rows)
    own_sums = slot_sums(lookup_grads, slot_index, slots * n_local)
    ordered = own_sums.reshape(n_local, n_group, capacity, 2 * width)
    ordered = jnp.transpose(ordered, (1, 0, 2, 3)).reshape(n_local * slots, 2 * width)
    received = lax.all_to_all(ordered, ("group", "local"), split_axis=0, concat_axis=0, tiled=True)
    arrived = jnp.sum(received.reshape(n_group, n_local, capacity, 2 * width), axis=1).reshape(
        slots, 2 * width
    )
    arrived_rows = lax.all_to_all(row_pairs, "group", split_axis=0, concat_axis=0, tiled=True)
    return apply_update(arrived, arrived_rows, tables, accums)


def solution(mesh):
    return jax.shard_map(
        local,
        mesh=mesh,
        in_specs=(
            P(("group", "local"), None),
            P(None, ("group", "local")),
            P(None, ("group", "local")),
            P(None, ("group", "local"), None),
            P(None, ("group", "local")),
        ),
        out_specs=(P(None, ("group", "local"), None), P(None, ("group", "local"))),
        check_vma=False,
    )
```

profile of v0, /device:TPU:1, one launch (start us, length us, event | category | flops | bytes accessed | tf_op | source)
XLA Modules:
  0.0 159.0 jit_solution(276250633649171804)
XLA Ops:
  2.0 6.0 %all-to-all-start = ((s32[8,16,2]{1,2,0:T(2,128)}), s32[8,16,2]{1,2,0:T(2,128)S(1)}, u32[]{:S(2)}, u32[]{:S(2)}) async-start(s32[8,16,2]{1,2,0:T(2,128)} %copy.11), calls=%async_computation | async-start | bytes 16384 | tf_op jit(solution)/shard_map/all_to_all | solution.py:70
  8.0 68.6 %while.12 = (s32[]{:T(128)}, f32[2048,512]{0,1:T(8,128)}, s32[4,2,2048]{2,1,0:T(2,128)}, bf16[4,2048,256]{2,1,0:T(8,128)(2,1)}, s32[]{:T(128)}, /*index=5*/s32[]{:T(128)}, s32[]{}) while((s32[]{:T(128)}, f32[2048,512]{0,1:T(8,128)}, s32[4,2,2048]{2,1,0:T(2,128)}, bf16[4,2048,256]{2,1,0:T(8,128)(2,1)}, s32[]{:T(128)}, ...), condition=%wide.region_1.2_spmd.clone.clone, body=%wide.region_0.1_spmd.clone.clone.sunk | while | flops 4306501632 | bytes 18924652 | solution.py:31
  8.0 0.8 constant_dynamic-slice_fusion.3
  8.8 4.8 %fusion.30 = f32[2048,256]{0,1:T(8,128)S(1)} fusion(s32[2048]{0:T(1024)S(1)} %bitcast.56, bf16[4,2048,256]{2,1,0:T(8,128)(2,1)} %get-tuple-element.130, s32[]{:T(128)} %get-tuple-element.120), kind=kOutput, calls=%fused_computation.6.clone.1 | convolution fusion | flops 2151677952 | bytes 3154432 | tf_op jit(solution)/shard_map/while/body/eval_jaxpr/dot_general | solution.py:24
  13.6 6.1 %fusion.31 = f32[2048,256]{0,1:T(8,128)} fusion(s32[2048]{0:T(1024)S(1)} %bitcast.55, bf16[4,2048,256]{2,1,0:T(8,128)(2,1)} %get-tuple-element.130, s32[]{:T(128)} %get-tuple-element.120), kind=kOutput, calls=%fused_computation.5.clone.1 | convolution fusion | flops 2151677952 | bytes 3154432 | tf_op jit(solution)/shard_map/while/body/eval_jaxpr/dot_general | solution.py:24
  19.7 4.5 %maximum_add_fusion.2 = f32[2048,512]{0,1:T(8,128)} fusion(f32[2048,256]{0,1:T(8,128)S(1)} %fusion.30, f32[2048,256]{0,1:T(8,128)} %fusion.31, f32[2048,512]{0,1:T(8,128)} %get-tuple-element.121, pred[]{:T(512)S(6)} %compare.5), kind=kLoop, calls=%fused_computation.9.clone.1 | loop fusion | flops 3145728 | bytes 12582913 | tf_op jit(solution)/shard_map/while/body/eval_jaxpr/add | solution.py:28
  25.0 4.8 %fusion.30 = f32[2048,256]{0,1:T(8,128)S(1)} fusion(s32[2048]{0:T(1024)S(1)} %bitcast.56, bf16[4,2048,256]{2,1,0:T(8,128)(2,1)} %get-tuple-element.130, s32[]{:T(128)} %get-tuple-element.120), kind=kOutput, calls=%fused_computation.6.clone.1 | convolution fusion | flops 2151677952 | bytes 3154432 | tf_op jit(solution)/shard_map/while/body/eval_jaxpr/dot_general | solution.py:24
  29.8 6.1 %fusion.31 = f32[2048,256]{0,1:T(8,128)} fusion(s32[2048]{0:T(1024)S(1)} %bitcast.55, bf16[4,2048,256]{2,1,0:T(8,128)(2,1)} %get-tuple-element.130, s32[]{:T(128)} %get-tuple-element.120), kind=kOutput, calls=%fused_computation.5.clone.1 | convolution fusion | flops 2151677952 | bytes 3154432 | tf_op jit(solution)/shard_map/while/body/eval_jaxpr/dot_general | solution.py:24
  35.9 5.8 %maximum_add_fusion.2 = f32[2048,512]{0,1:T(8,128)} fusion(f32[2048,256]{0,1:T(8,128)S(1)} %fusion.30, f32[2048,256]{0,1:T(8,128)} %fusion.31, f32[2048,512]{0,1:T(8,128)} %get-tuple-element.121, pred[]{:T(512)S(6)} %compare.5), kind=kLoop, calls=%fused_computation.9.clone.1 | loop fusion | flops 3145728 | bytes 12582913 | tf_op jit(solution)/shard_map/while/body/eval_jaxpr/add | solution.py:28
  42.5 4.8 %fusion.30 = f32[2048,256]{0,1:T(8,128)S(1)} fusion(s32[2048]{0:T(1024)S(1)} %bitcast.56, bf16[4,2048,256]{2,1,0:T(8,128)(2,1)} %get-tuple-element.130, s32[]{:T(128)} %get-tuple-element.120), kind=kOutput, calls=%fused_computation.6.clone.1 | convolution fusion | flops 2151677952 | bytes 3154432 | tf_op jit(solution)/shard_map/while/body/eval_jaxpr/dot_general | solution.py:24
  47.2 6.1 %fusion.31 = f32[2048,256]{0,1:T(8,128)} fusion(s32[2048]{0:T(1024)S(1)} %bitcast.55, bf16[4,2048,256]{2,1,0:T(8,128)(2,1)} %get-tuple-element.130, s32[]{:T(128)} %get-tuple-element.120), kind=kOutput, calls=%fused_computation.5.clone.1 | convolution fusion | flops 2151677952 | bytes 3154432 | tf_op jit(solution)/shard_map/while/body/eval_jaxpr/dot_general | solution.py:24
  53.3 5.8 %maximum_add_fusion.2 = f32[2048,512]{0,1:T(8,128)} fusion(f32[2048,256]{0,1:T(8,128)S(1)} %fusion.30, f32[2048,256]{0,1:T(8,128)} %fusion.31, f32[2048,512]{0,1:T(8,128)} %get-tuple-element.121, pred[]{:T(512)S(6)} %compare.5), kind=kLoop, calls=%fused_computation.9.clone.1 | loop fusion | flops 3145728 | bytes 12582913 | tf_op jit(solution)/shard_map/while/body/eval_jaxpr/add | solution.py:28
  59.9 4.8 %fusion.30 = f32[2048,256]{0,1:T(8,128)S(1)} fusion(s32[2048]{0:T(1024)S(1)} %bitcast.56, bf16[4,2048,256]{2,1,0:T(8,128)(2,1)} %get-tuple-element.130, s32[]{:T(128)} %get-tuple-element.120), kind=kOutput, calls=%fused_computation.6.clone.1 | convolution fusion | flops 2151677952 | bytes 3154432 | tf_op jit(solution)/shard_map/while/body/eval_jaxpr/dot_general | solution.py:24
  64.7 6.1 %fusion.31 = f32[2048,256]{0,1:T(8,128)} fusion(s32[2048]{0:T(1024)S(1)} %bitcast.55, bf16[4,2048,256]{2,1,0:T(8,128)(2,1)} %get-tuple-element.130, s32[]{:T(128)} %get-tuple-element.120), kind=kOutput, calls=%fused_computation.5.clone.1 | convolution fusion | flops 2151677952 | bytes 3154432 | tf_op jit(solution)/shard_map/while/body/eval_jaxpr/dot_general | solution.py:24
  70.8 5.8 %maximum_add_fusion.2 = f32[2048,512]{0,1:T(8,128)} fusion(f32[2048,256]{0,1:T(8,128)S(1)} %fusion.30, f32[2048,256]{0,1:T(8,128)} %fusion.31, f32[2048,512]{0,1:T(8,128)} %get-tuple-element.121, pred[]{:T(512)S(6)} %compare.5), kind=kLoop, calls=%fused_computation.9.clone.1 | loop fusion | flops 3145728 | bytes 12582913 | tf_op jit(solution)/shard_map/while/body/eval_jaxpr/add | solution.py:28
  76.6 5.3 %copy.13 = f32[2048,512]{1,0:T(8,128)} copy(f32[2048,512]{0,1:T(8,128)} %get-tuple-element.32) | data formatting | bytes 8388608 | tf_op jit(solution)/shard_map/while | solution.py:31
  81.9 5.0 %copy.14 = f32[8,16,16,512]{3,2,1,0:T(8,128)} copy(f32[8,16,16,512]{3,2,0,1:T(8,128)} %bitcast.52) | data formatting | bytes 8388608 | tf_op jit(solution)/shard_map/transpose | solution.py:65
  86.9 10.8 %all-to-all-start.1 = ((f32[128,16,512]{2,1,0:T(8,128)}), f32[128,16,512]{2,1,0:T(8,128)}, u32[]{:S(2)}, u32[]{:S(2)}) async-start(f32[128,16,512]{2,1,0:T(8,128)} %bitcast.51), calls=%async_computation.1 | async-start | bytes 8388608 | tf_op jit(solution)/shard_map/all_to_all | solution.py:66
  97.8 51.1 %all-to-all-done.1 = f32[128,16,512]{2,1,0:T(8,128)} async-done(((f32[128,16,512]{2,1,0:T(8,128)}), f32[128,16,512]{2,1,0:T(8,128)}, u32[]{:S(2)}, u32[]{:S(2)}) %all-to-all-start.1) | async-done | bytes 4194336 | tf_op jit(solution)/shard_map/all_to_all | solution.py:66
  148.8 2.6 %bitcast_reduce_fusion = f32[8,16,512]{2,1,0:T(8,128)S(1)} fusion(f32[128,16,512]{2,1,0:T(8,128)} %all-to-all-done.1), kind=kLoop, calls=%fused_computation.18 | loop fusion | flops 983040 | bytes 4456448 | tf_op jit(solution)/shard_map/reduce_sum | solution.py:67
  151.5 1.5 scatter_custom_fusion
  153.2 1.5 scatter_custom_fusion.1
  155.0 1.9 %fusion.13 = (f32[1,1024,256]{2,1,0:T(8,128)S(1)}, f32[1,1024,256]{2,1,0:T(8,128)S(1)}) fusion(f32[1024,256]{1,0:T(8,128)S(1)} %scatter_custom_fusion, f32[2,1024,256]{2,1,0:T(8,128)} %param.10, f32[1024]{0:T(1024)S(1)} %get-tuple-element.83, f32[1024]{0:T(1024)S(1)} %get-tuple-element.82, f32[1024,256]{1,0:T(8,128)S(1)} %scatter_custom_fusion.1), kind=kLoop, calls=%fused_computation.23 | loop fusion | flops 1572864 | bytes 6299648 | tf_op jit(solution)/shard_map/stack | solution.py:53
  156.9 1.5 pad_maximum_fusion
  (19 shorter events, 5.0 us)
Async XLA Ops:
  2.0 84.9 %all-to-all-start = ((s32[8,16,2]{1,2,0:T(2,128)}), s32[8,16,2]{1,2,0:T(2,128)S(1)}, u32[]{:S(2)}, u32[]{:S(2)}) async-start(s32[8,16,2]{1,2,0:T(2,128)} %copy.11), calls=%async_computation | async-start | bytes 16384 | tf_op jit(solution)/shard_map/all_to_all | solution.py:70
  86.9 62.0 %all-to-all-start.1 = ((f32[128,16,512]{2,1,0:T(8,128)}), f32[128,16,512]{2,1,0:T(8,128)}, u32[]{:S(2)}, u32[]{:S(2)}) async-start(f32[128,16,512]{2,1,0:T(8,128)} %bitcast.51), calls=%async_computation.1 | async-start | bytes 8388608 | tf_op jit(solution)/shard_map/all_to_all | solution.py:66
  97.8 57.2 %copy-start = (f32[2,1024]{1,0:T(2,128)S(1)}, f32[2,1024]{1,0:T(2,128)}, u32[]{:S(2)}) copy-start(f32[2,1024]{1,0:T(2,128)} %param.11) | copy-start | bytes 24580
where the time goes:
time: 160 us; the launch traced here: 159 us
  waiting for transfers between devices  51.1 us (32%)
  matrix products  43.5 us (27%)
  other arithmetic  31.9 us (20%)
  starting transfers between devices  16.8 us (10%)
  local copies, waits for them, and re-layouts  15 us (9%)
    all_to_all x1, waiting for transfers between devices, local(): lax.all_to_all(ordered, ('group', 'local'), split_axis=0, concat_axis=0,...  51.1 us
    dot_general x8, matrix products, accumulate(): lax.dot_general(onehot, gradients, (((0,), (0,)), ((), ())), preferred_el...  43.5 us
    add x4, other arithmetic, accumulate(): return (running + jnp.concatenate(pieces, axis=1), None)  21.8 us
    all_to_all x1, starting transfers between devices, local(): lax.all_to_all(ordered, ('group', 'local'), split_axis=0, concat_axis=0,...  10.8 us
    all_to_all x1, starting transfers between devices, local(): lax.all_to_all(row_pairs, 'group', split_axis=0, concat_axis=0, tiled=True)  5.97 us
    while x1, local copies, waits for them, and re-layouts, slot_sums(): summed, _ = lax.scan(accumulate, start_sums, (grad_blocks, index_blocks))  5.34 us
    transpose x1, local copies, waits for them, and re-layouts, local(): jnp.transpose(ordered, (1, 0, 2, 3)).reshape(n_local * slots, 2 * width)  4.95 us
    another operation x3, other arithmetic, apply_update(): return (jnp.stack(new_tables), jnp.stack(new_accums))  3.95 us
  transfers between devices with their start and end apart: 2, of which 1 were waited for; matrix products, arithmetic and copies ran while one was open for 50% of the time, Pallas kernels for 0%

commit v1 on v0

--- a/solution.py
+++ b/solution.py
@@ -67,7 +67,20 @@
     arrived = jnp.sum(received.reshape(n_group, n_local, capacity, 2 * width), axis=1).reshape(
         slots, 2 * width
     )
-    arrived_rows = lax.all_to_all(row_pairs, "group", split_axis=0, concat_axis=0, tiled=True)
+    ways, here = (lax.axis_size("group"), lax.axis_index("group"))
+    width_2 = row_pairs.shape[0] // ways
+    dims = list(row_pairs.shape)
+    dims[0] = width_2
+    height = dims[0]
+    dims[0] = height * ways
+    arrived_rows = jnp.zeros(dims, row_pairs.dtype)
+    for mask in range(ways):
+        part = lax.dynamic_slice_in_dim(row_pairs, (here ^ mask) * width_2, width_2, axis=0)
+        if mask:
+            part = lax.ppermute(part, "group", [(d, d ^ mask) for d in range(ways)])
+        arrived_rows = lax.dynamic_update_slice_in_dim(
+            arrived_rows, part, (here ^ mask) * height, axis=0
+        )
     return apply_update(arrived, arrived_rows, tables, accums)
 
 

time: 160 us -> 141 us (0.88)
  other arithmetic: 31.9 us -> 16.1 us
  waiting for transfers between devices: 51.1 us -> 40.9 us
  local copies, waits for them, and re-layouts: 15 us -> 23.2 us
  matrix products: 43.5 us -> 38.8 us
  starting transfers between devices: 16.8 us -> 20.5 us
    all_to_all x1, waiting for transfers between devices: 51.1 us -> 0.59 us  [local(): lax.all_to_all(ordered, ('group', 'local'), split_axis=0, concat_axis=0,...]
    ppermute x0 -> x7, waiting for transfers between devices: none -> 40.3 us  [local(): part = lax.ppermute(part, 'group', [(d, d ^ mask) for d in range(ways)])]
    add x4, other arithmetic: 21.8 us -> 5.96 us  [accumulate(): return (running + jnp.concatenate(pieces, axis=1), None)]
    ppermute x0 -> x7, starting transfers between devices: none -> 8.52 us  [local(): part = lax.ppermute(part, 'group', [(d, d ^ mask) for d in range(ways)])]
    while x0 -> x16, local copies, waits for them, and re-layouts: none -> 7.9 us
    all_to_all x1 -> x0, starting transfers between devices: 5.97 us -> none  [local(): lax.all_to_all(row_pairs, 'group', split_axis=0, concat_axis=0, tiled=True)]
    dot_general x8, matrix products: 43.5 us -> 38.8 us  [accumulate(): lax.dot_general(onehot, gradients, (((0,), (0,)), ((), ())), preferred_el...]
  transfers between devices with their start and end apart: 2 -> 8, of which waited for: 1 -> 5; matrix products, arithmetic and copies ran while one was open for 50% -> 1% of each run, Pallas kernels for 0% -> 0%
where the time goes in v1:
time: 141 us; the launch traced here: 140 us
  waiting for transfers between devices  40.9 us (29%)
  matrix products  38.8 us (28%)
  local copies, waits for them, and re-layouts  23.2 us (16%)
  starting transfers between devices  20.5 us (15%)
  other arithmetic  16.1 us (11%)
    ppermute x7, waiting for transfers between devices, local(): part = lax.ppermute(part, 'group', [(d, d ^ mask) for d in range(ways)])  40.3 us
    dot_general x8, matrix products, accumulate(): lax.dot_general(onehot, gradients, (((0,), (0,)), ((), ())), preferred_el...  38.8 us
    all_to_all x1, starting transfers between devices, local(): lax.all_to_all(ordered, ('group', 'local'), split_axis=0, concat_axis=0,...  12 us
    ppermute x7, starting transfers between devices, local(): part = lax.ppermute(part, 'group', [(d, d ^ mask) for d in range(ways)])  8.52 us
    while x16, local copies, waits for them, and re-layouts  7.9 us
    add x4, other arithmetic, accumulate(): return (running + jnp.concatenate(pieces, axis=1), None)  5.96 us
    while x1, local copies, waits for them, and re-layouts, slot_sums(): summed, _ = lax.scan(accumulate, start_sums, (grad_blocks, index_blocks))  5.35 us
    transpose x1, local copies, waits for them, and re-layouts, local(): jnp.transpose(ordered, (1, 0, 2, 3)).reshape(n_local * slots, 2 * width)  5 us
  transfers between devices with their start and end apart: 8, of which 5 were waited for; matrix products, arithmetic and copies ran while one was open for 1% of the time, Pallas kernels for 0%

profile of v1, /device:TPU:1, one launch (start us, length us, event | category | flops | bytes accessed | tf_op | source)
XLA Modules:
  0.0 140.4 jit_solution(12140327442248434260)
XLA Ops:
  0.6 56.1 %while.12 = (s32[]{:T(128)}, f32[2048,512]{0,1:T(8,128)}, s32[4,2,2048]{2,1,0:T(2,128)}, bf16[4,2048,256]{2,1,0:T(8,128)(2,1)}, s32[]{:T(128)}, /*index=5*/s32[]{:T(128)}, s32[]{}) while((s32[]{:T(128)}, f32[2048,512]{0,1:T(8,128)}, s32[4,2,2048]{2,1,0:T(2,128)}, bf16[4,2048,256]{2,1,0:T(8,128)(2,1)}, s32[]{:T(128)}, ...), condition=%wide.region_1.2_spmd.clone.clone, body=%wide.region_0.1_spmd.clone.clone.sunk | while | flops 4306501632 | bytes 52478128 | solution.py:31
  1.5 4.8 %fusion.39 = f32[2048,256]{0,1:T(8,128)S(1)} fusion(s32[2048]{0:T(1024)S(1)} %bitcast.67, bf16[4,2048,256]{2,1,0:T(8,128)(2,1)} %get-tuple-element.138, s32[]{:T(128)S(6)} %copy.19), kind=kOutput, calls=%fused_computation.5.clone.1 | convolution fusion | flops 2151677952 | bytes 3153924 | tf_op jit(solution)/shard_map/while/body/eval_jaxpr/dot_general | solution.py:24
  6.3 4.9 %fusion.38 = f32[2048,256]{0,1:T(8,128)S(1)} fusion(s32[2048]{0:T(1024)S(1)} %bitcast.66, bf16[4,2048,256]{2,1,0:T(8,128)(2,1)} %get-tuple-element.138, s32[]{:T(128)S(6)} %copy.19), kind=kOutput, calls=%fused_computation.6.clone.1 | convolution fusion | flops 2151677952 | bytes 3153924 | tf_op jit(solution)/shard_map/while/body/eval_jaxpr/dot_general | solution.py:24
  12.7 2.0 %copy-done.1 = f32[2048,512]{0,1:T(8,128)} copy-done((f32[2048,512]{0,1:T(8,128)}, f32[2048,512]{0,1:T(8,128)S(1)}, u32[]{:S(2)}) %copy-start.1) | copy-done | bytes 4194328 | tf_op jit(solution)/shard_map/while
  15.5 4.8 %fusion.39 = f32[2048,256]{0,1:T(8,128)S(1)} fusion(s32[2048]{0:T(1024)S(1)} %bitcast.67, bf16[4,2048,256]{2,1,0:T(8,128)(2,1)} %get-tuple-element.138, s32[]{:T(128)S(6)} %copy.19), kind=kOutput, calls=%fused_computation.5.clone.1 | convolution fusion | flops 2151677952 | bytes 3153924 | tf_op jit(solution)/shard_map/while/body/eval_jaxpr/dot_general | solution.py:24
  20.3 4.9 %fusion.38 = f32[2048,256]{0,1:T(8,128)S(1)} fusion(s32[2048]{0:T(1024)S(1)} %bitcast.66, bf16[4,2048,256]{2,1,0:T(8,128)(2,1)} %get-tuple-element.138, s32[]{:T(128)S(6)} %copy.19), kind=kOutput, calls=%fused_computation.6.clone.1 | convolution fusion | flops 2151677952 | bytes 3153924 | tf_op jit(solution)/shard_map/while/body/eval_jaxpr/dot_general | solution.py:24
  26.7 2.0 %copy-done.1 = f32[2048,512]{0,1:T(8,128)} copy-done((f32[2048,512]{0,1:T(8,128)}, f32[2048,512]{0,1:T(8,128)S(1)}, u32[]{:S(2)}) %copy-start.1) | copy-done | bytes 4194328 | tf_op jit(solution)/shard_map/while
  29.5 4.8 %fusion.39 = f32[2048,256]{0,1:T(8,128)S(1)} fusion(s32[2048]{0:T(1024)S(1)} %bitcast.67, bf16[4,2048,256]{2,1,0:T(8,128)(2,1)} %get-tuple-element.138, s32[]{:T(128)S(6)} %copy.19), kind=kOutput, calls=%fused_computation.5.clone.1 | convolution fusion | flops 2151677952 | bytes 3153924 | tf_op jit(solution)/shard_map/while/body/eval_jaxpr/dot_general | solution.py:24
  34.3 4.9 %fusion.38 = f32[2048,256]{0,1:T(8,128)S(1)} fusion(s32[2048]{0:T(1024)S(1)} %bitcast.66, bf16[4,2048,256]{2,1,0:T(8,128)(2,1)} %get-tuple-element.138, s32[]{:T(128)S(6)} %copy.19), kind=kOutput, calls=%fused_computation.6.clone.1 | convolution fusion | flops 2151677952 | bytes 3153924 | tf_op jit(solution)/shard_map/while/body/eval_jaxpr/dot_general | solution.py:24
  40.8 2.0 %copy-done.1 = f32[2048,512]{0,1:T(8,128)} copy-done((f32[2048,512]{0,1:T(8,128)}, f32[2048,512]{0,1:T(8,128)S(1)}, u32[]{:S(2)}) %copy-start.1) | copy-done | bytes 4194328 | tf_op jit(solution)/shard_map/while
  43.5 4.8 %fusion.39 = f32[2048,256]{0,1:T(8,128)S(1)} fusion(s32[2048]{0:T(1024)S(1)} %bitcast.67, bf16[4,2048,256]{2,1,0:T(8,128)(2,1)} %get-tuple-element.138, s32[]{:T(128)S(6)} %copy.19), kind=kOutput, calls=%fused_computation.5.clone.1 | convolution fusion | flops 2151677952 | bytes 3153924 | tf_op jit(solution)/shard_map/while/body/eval_jaxpr/dot_general | solution.py:24
  48.3 4.9 %fusion.38 = f32[2048,256]{0,1:T(8,128)S(1)} fusion(s32[2048]{0:T(1024)S(1)} %bitcast.66, bf16[4,2048,256]{2,1,0:T(8,128)(2,1)} %get-tuple-element.138, s32[]{:T(128)S(6)} %copy.19), kind=kOutput, calls=%fused_computation.6.clone.1 | convolution fusion | flops 2151677952 | bytes 3153924 | tf_op jit(solution)/shard_map/while/body/eval_jaxpr/dot_general | solution.py:24
  54.8 2.0 %copy-done.1 = f32[2048,512]{0,1:T(8,128)} copy-done((f32[2048,512]{0,1:T(8,128)}, f32[2048,512]{0,1:T(8,128)S(1)}, u32[]{:S(2)}) %copy-start.1) | copy-done | bytes 4194328 | tf_op jit(solution)/shard_map/while
  56.7 5.3 %copy.7 = f32[2048,512]{1,0:T(8,128)} copy(f32[2048,512]{0,1:T(8,128)} %get-tuple-element.32) | data formatting | bytes 8388608 | tf_op jit(solution)/shard_map/while | solution.py:31
  62.1 5.0 %copy.8 = f32[8,16,16,512]{3,2,1,0:T(8,128)} copy(f32[8,16,16,512]{3,2,0,1:T(8,128)} %bitcast.63) | data formatting | bytes 8388608 | tf_op jit(solution)/shard_map/transpose | solution.py:65
  67.1 12.0 %all-to-all-start = ((f32[128,16,512]{2,1,0:T(8,128)}), f32[128,16,512]{2,1,0:T(8,128)}, u32[]{:S(2)}, u32[]{:S(2)}) async-start(f32[128,16,512]{2,1,0:T(8,128)} %bitcast.62), calls=%async_computation | async-start | bytes 8388608 | tf_op jit(solution)/shard_map/all_to_all | solution.py:66
  79.2 2.9 %collective-permute-start.6 = (s32[16,2]{0,1:T(2,128)S(1)}, s32[16,2]{0,1:T(2,128)S(1)}, u32[]{:S(2)}, u32[]{:S(2)}) collective-permute-start(s32[16,2]{0,1:T(2,128)S(1)} %get-tuple-element.82), channel_id=1, source_target_pairs={{0,112},{16,96},{32,80},{48,64},{64,48},{80,32},{96,16},{112,0},{1... | collective-permute-start | bytes 392 | tf_op jit(solution)/shard_map/ppermute | solution.py:80
  82.7 2.4 %collective-permute-start.3 = (s32[16,2]{0,1:T(2,128)S(1)}, s32[16,2]{0,1:T(2,128)S(1)}, u32[]{:S(2)}, u32[]{:S(2)}) collective-permute-start(s32[16,2]{0,1:T(2,128)S(1)} %get-tuple-element.84), channel_id=1, source_target_pairs={{0,64},{16,80},{32,96},{48,112},{64,0},{80,16},{96,32},{112,48},{1... | collective-permute-start | bytes 392 | tf_op jit(solution)/shard_map/ppermute | solution.py:80
  86.8 1.7 %collective-permute-start.2 = (s32[16,2]{0,1:T(2,128)S(1)}, s32[16,2]{0,1:T(2,128)S(1)}, u32[]{:S(2)}, u32[]{:S(2)}) collective-permute-start(s32[16,2]{0,1:T(2,128)S(1)} %get-tuple-element.85), channel_id=1, source_target_pairs={{0,48},{16,32},{32,16},{48,0},{64,112},{80,96},{96,80},{112,64},{1... | collective-permute-start | bytes 392 | tf_op jit(solution)/shard_map/ppermute | solution.py:80
  88.6 36.4 %collective-permute-done.1 = s32[16,2]{0,1:T(2,128)S(1)} collective-permute-done((s32[16,2]{0,1:T(2,128)S(1)}, s32[16,2]{0,1:T(2,128)S(1)}, u32[]{:S(2)}, u32[]{:S(2)}) %collective-permute-start.1) | collective-permute-done | bytes 160 | tf_op jit(solution)/shard_map/ppermute | solution.py:80
  126.9 2.3 %collective-permute-done.5 = s32[16,2]{0,1:T(2,128)S(1)} collective-permute-done((s32[16,2]{0,1:T(2,128)S(1)}, s32[16,2]{0,1:T(2,128)S(1)}, u32[]{:S(2)}, u32[]{:S(2)}) %collective-permute-start.5) | collective-permute-done | bytes 160 | tf_op jit(solution)/shard_map/ppermute | solution.py:80
  130.2 2.6 %bitcast_reduce_fusion = f32[8,16,512]{2,1,0:T(8,128)S(1)} fusion(f32[128,16,512]{2,1,0:T(8,128)} %all-to-all-done), kind=kLoop, calls=%fused_computation.18 | loop fusion | flops 983040 | bytes 4456448 | tf_op jit(solution)/shard_map/reduce_sum | solution.py:67
  132.9 1.5 %scatter_custom_fusion.1 = f32[1024,256]{1,0:T(8,128)S(1)} fusion(s32[128]{0:T(128)S(1)} %get-tuple-element.81, f32[]{:T(128)} %constant.22.clone.1, f32[128,512]{1,0:T(8,128)S(1)} %bitcast.64), kind=kCustom, calls=%fused_computation.26 | custom fusion | flops 32768 | bytes 1179652 | tf_op jit(solution)/shard_map/scatter-add | solution.py:45
  137.0 1.9 %fusion.13 = (f32[1,1024,256]{2,1,0:T(8,128)S(1)}, f32[1,1024,256]{2,1,0:T(8,128)S(1)}) fusion(f32[1024,256]{1,0:T(8,128)S(1)} %scatter_custom_fusion, f32[2,1024,256]{2,1,0:T(8,128)} %param.10, f32[1024]{0:T(1024)S(1)} %get-tuple-element.91, f32[1024]{0:T(1024)S(1)} %get-tuple-element.90, f32[1024,256]{1,0:T(8,128)S(1)} %scatter_custom_fusion.1), kind=kLoop, calls=%fused_computation.23 | loop fusion | flops 1572864 | bytes 6299648 | tf_op jit(solution)/shard_map/stack | solution.py:53
  (55 shorter events, 18.5 us)
Async XLA Ops:
  6.3 4.9 %copy-start = (f32[2048,512]{0,1:T(8,128)S(1)}, f32[2048,512]{0,1:T(8,128)}, u32[]{:S(2)}) copy-start(f32[2048,512]{0,1:T(8,128)} %get-tuple-element.129) | copy-start | bytes 12582916 | tf_op jit(solution)/shard_map/while
  12.7 2.0 %copy-start.1 = (f32[2048,512]{0,1:T(8,128)}, f32[2048,512]{0,1:T(8,128)S(1)}, u32[]{:S(2)}) copy-start(f32[2048,512]{0,1:T(8,128)S(1)} %maximum_add_fusion.2) | copy-start | bytes 12582916 | tf_op jit(solution)/shard_map/while
  20.3 4.9 %copy-start = (f32[2048,512]{0,1:T(8,128)S(1)}, f32[2048,512]{0,1:T(8,128)}, u32[]{:S(2)}) copy-start(f32[2048,512]{0,1:T(8,128)} %get-tuple-element.129) | copy-start | bytes 12582916 | tf_op jit(solution)/shard_map/while
  26.7 2.0 %copy-start.1 = (f32[2048,512]{0,1:T(8,128)}, f32[2048,512]{0,1:T(8,128)S(1)}, u32[]{:S(2)}) copy-start(f32[2048,512]{0,1:T(8,128)S(1)} %maximum_add_fusion.2) | copy-start | bytes 12582916 | tf_op jit(solution)/shard_map/while
  34.3 4.9 %copy-start = (f32[2048,512]{0,1:T(8,128)S(1)}, f32[2048,512]{0,1:T(8,128)}, u32[]{:S(2)}) copy-start(f32[2048,512]{0,1:T(8,128)} %get-tuple-element.129) | copy-start | bytes 12582916 | tf_op jit(solution)/shard_map/while
  40.7 2.0 %copy-start.1 = (f32[2048,512]{0,1:T(8,128)}, f32[2048,512]{0,1:T(8,128)S(1)}, u32[]{:S(2)}) copy-start(f32[2048,512]{0,1:T(8,128)S(1)} %maximum_add_fusion.2) | copy-start | bytes 12582916 | tf_op jit(solution)/shard_map/while
  48.3 4.9 %copy-start = (f32[2048,512]{0,1:T(8,128)S(1)}, f32[2048,512]{0,1:T(8,128)}, u32[]{:S(2)}) copy-start(f32[2048,512]{0,1:T(8,128)} %get-tuple-element.129) | copy-start | bytes 12582916 | tf_op jit(solution)/shard_map/while
  54.8 2.0 %copy-start.1 = (f32[2048,512]{0,1:T(8,128)}, f32[2048,512]{0,1:T(8,128)S(1)}, u32[]{:S(2)}) copy-start(f32[2048,512]{0,1:T(8,128)S(1)} %maximum_add_fusion.2) | copy-start | bytes 12582916 | tf_op jit(solution)/shard_map/while
  67.1 12.0 %copy-start.2 = (s32[2,128]{1,0:T(2,128)S(1)}, s32[2,128]{1,0:T(2,128)}, u32[]{:S(2)}) copy-start(s32[2,128]{1,0:T(2,128)} %param.9) | copy-start | bytes 3076
  67.1 63.1 %all-to-all-start = ((f32[128,16,512]{2,1,0:T(8,128)}), f32[128,16,512]{2,1,0:T(8,128)}, u32[]{:S(2)}, u32[]{:S(2)}) async-start(f32[128,16,512]{2,1,0:T(8,128)} %bitcast.62), calls=%async_computation | async-start | bytes 8388608 | tf_op jit(solution)/shard_map/all_to_all | solution.py:66
  79.2 50.2 %collective-permute-start.6 = (s32[16,2]{0,1:T(2,128)S(1)}, s32[16,2]{0,1:T(2,128)S(1)}, u32[]{:S(2)}, u32[]{:S(2)}) collective-permute-start(s32[16,2]{0,1:T(2,128)S(1)} %get-tuple-element.82), channel_id=1, source_target_pairs={{0,112},{16,96},{32,80},{48,64},{64,48},{80,32},{96,16},{112,0},{1... | collective-permute-start | bytes 392 | tf_op jit(solution)/shard_map/ppermute | solution.py:80
  82.1 44.5 %collective-permute-start.4 = (s32[16,2]{0,1:T(2,128)S(1)}, s32[16,2]{0,1:T(2,128)S(1)}, u32[]{:S(2)}, u32[]{:S(2)}) collective-permute-start(s32[16,2]{0,1:T(2,128)S(1)} %get-tuple-element.83), channel_id=1, source_target_pairs={{0,80},{16,64},{32,112},{48,96},{64,16},{80,0},{96,48},{112,32},{1... | collective-permute-start | bytes 392 | tf_op jit(solution)/shard_map/ppermute | solution.py:80
  82.7 43.7 %collective-permute-start.3 = (s32[16,2]{0,1:T(2,128)S(1)}, s32[16,2]{0,1:T(2,128)S(1)}, u32[]{:S(2)}, u32[]{:S(2)}) collective-permute-start(s32[16,2]{0,1:T(2,128)S(1)} %get-tuple-element.84), channel_id=1, source_target_pairs={{0,64},{16,80},{32,96},{48,112},{64,0},{80,16},{96,32},{112,48},{1... | collective-permute-start | bytes 392 | tf_op jit(solution)/shard_map/ppermute | solution.py:80
  85.1 39.9 %collective-permute-start.1 = (s32[16,2]{0,1:T(2,128)S(1)}, s32[16,2]{0,1:T(2,128)S(1)}, u32[]{:S(2)}, u32[]{:S(2)}) collective-permute-start(s32[16,2]{0,1:T(2,128)S(1)} %get-tuple-element.86), channel_id=1, source_target_pairs={{0,32},{16,48},{32,0},{48,16},{64,96},{80,112},{96,64},{112,80},{1... | collective-permute-start | bytes 392 | tf_op jit(solution)/shard_map/ppermute | solution.py:80
  85.1 1.6 %collective-permute-start = (s32[16,2]{0,1:T(2,128)S(1)}, s32[16,2]{0,1:T(2,128)S(1)}, u32[]{:S(2)}, u32[]{:S(2)}) collective-permute-start(s32[16,2]{0,1:T(2,128)S(1)} %get-tuple-element.87), channel_id=1, source_target_pairs={{0,16},{16,0},{32,48},{48,32},{64,80},{80,64},{96,112},{112,96},{1... | collective-permute-start | bytes 392 | tf_op jit(solution)/shard_map/ppermute | solution.py:80
  86.8 39.4 %collective-permute-start.2 = (s32[16,2]{0,1:T(2,128)S(1)}, s32[16,2]{0,1:T(2,128)S(1)}, u32[]{:S(2)}, u32[]{:S(2)}) collective-permute-start(s32[16,2]{0,1:T(2,128)S(1)} %get-tuple-element.85), channel_id=1, source_target_pairs={{0,48},{16,32},{32,16},{48,0},{64,112},{80,96},{96,80},{112,64},{1... | collective-permute-start | bytes 392 | tf_op jit(solution)/shard_map/ppermute | solution.py:80
  125.0 4.1 %collective-permute-start.5 = (s32[16,2]{0,1:T(2,128)S(1)}, s32[16,2]{0,1:T(2,128)S(1)}, u32[]{:S(2)}, u32[]{:S(2)}) collective-permute-start(s32[16,2]{0,1:T(2,128)S(1)} %get-tuple-element.89), channel_id=1, source_target_pairs={{0,96},{16,112},{32,64},{48,80},{64,32},{80,48},{96,0},{112,16},{1... | collective-permute-start | bytes 392 | tf_op jit(solution)/shard_map/ppermute | solution.py:80
  129.6 6.8 %copy-start.3 = (f32[2,1024]{1,0:T(2,128)S(1)}, f32[2,1024]{1,0:T(2,128)}, u32[]{:S(2)}) copy-start(f32[2,1024]{1,0:T(2,128)} %param.11) | copy-start | bytes 24580
